TPU v7x, 32 devices: a whole 2x2x4 slice. The times are simulated.
32 devices in a mesh: dp: 8 (over z, y), mix: 4 (over x, core).
Axes of the slice: x: 2, y: 2, z: 4, core: 2. Of those that a mesh axis runs over, the one named last changes fastest.
Arguments:
- patches: bfloat16 [224, 196, 768], P('dp', 'mix'), may hold values from -6 to 6
- valid_counts: int32 [8], P('dp'), may hold values from 7 to 28, as said below
- gain_one: float32 [768], replicated, may hold values from 0.5 to 1.5
- shift_one: float32 [768], replicated, may hold values from -1.25 to 1.25
- tok_in: bfloat16 [196, 384], replicated, may hold values from -0.4375 to 0.4375
- tok_inbias: float32 [384], replicated, may hold values from -1.25 to 1.25
- tok_out: bfloat16 [384, 196], replicated, may hold values from -0.3125 to 0.3125
- tok_outbias: float32 [196], replicated, may hold values from -1.25 to 1.25
- gain_two: float32 [768], replicated, may hold values from 0.5 to 1.5
- shift_two: float32 [768], replicated, may hold values from -1.25 to 1.25
- chan_in: bfloat16 [768, 3072], replicated, may hold values from -0.21875 to 0.21875
- chan_inbias: float32 [3072], replicated, may hold values from -1.25 to 1.25
- chan_out: bfloat16 [3072, 768], replicated, may hold values from -0.109375 to 0.109375
- chan_outbias: float32 [768], replicated, may hold values from -1.25 to 1.25
- out_grad: bfloat16 [224, 196, 768], P('dp', 'mix'), may hold values from -6 to 6
Outputs:
- mixed_out: bfloat16 [224, 196, 768], P('dp', 'mix')
- patch_grad: bfloat16 [224, 196, 768], P('dp', 'mix')
- grad_gain_one: float32 [768], replicated
- grad_shift_one: float32 [768], replicated
- grad_tok_in: float32 [196, 384], replicated
- grad_tok_inbias: float32 [384], replicated
- grad_tok_out: float32 [384, 196], replicated
- grad_tok_outbias: float32 [196], replicated
- grad_gain_two: float32 [768], replicated
- grad_shift_two: float32 [768], replicated
- grad_chan_in: float32 [768, 3072], replicated
- grad_chan_inbias: float32 [3072], replicated
- grad_chan_out: float32 [3072, 768], replicated
- grad_chan_outbias: float32 [768], replicated
Inputs may be any that keep to these rules, and one draw needn't show every extreme that they name: `valid_counts`: how many of the 28 images of each index of dp are real; the rest are padding and get no gradient.
All inputs are finite; a program needn't handle non-finite values.
Results may differ from a plain program's by a relative error of at most 0.008.
Values may be sent and summed in bfloat16 or wider, within the bound.
A program may use at most 192 MiB of HBM per device.

v0:
```python
import jax
import jax.numpy as jnp
from jax import lax
from jax.sharding import PartitionSpec as P

EPS = 1e-06


def layer_norm(values, gain, shift):
    center = values - jnp.mean(values, axis=-1, keepdims=True)
    spread = jnp.mean(center * center, axis=-1, keepdims=True)
    return center * lax.rsqrt(spread + EPS) * gain + shift


def shards(
    patches,
    valid_counts,
    gain_one,
    shift_one,
    tok_in,
    tok_inbias,
    tok_out,
    tok_outbias,
    gain_two,
    shift_two,
    chan_in,
    chan_inbias,
    chan_out,
    chan_outbias,
    out_grad,
):
    images, part, width = patches.shape
    rowcount = images * part
    inputs = patches.astype(jnp.float32)
    normed_full, first_back = jax.vjp(layer_norm, inputs, gain_one, shift_one)
    normed = normed_full.astype(jnp.bfloat16)
    columns = lax.all_to_all(normed, "mix", split_axis=2, concat_axis=1, tiled=True)
    widened = (
        jnp.einsum("bsc,sk->bkc", columns, tok_in, preferred_element_type=jnp.float32)
        + tok_inbias[None, :, None]
    )
    hidden = jax.nn.gelu(widened).astype(jnp.bfloat16)
    mixed_cols = (
        jnp.einsum("bkc,ks->bsc", hidden, tok_out, preferred_element_type=jnp.float32)
        + tok_outbias[None, :, None]
    ).astype(jnp.bfloat16)
    mixed = lax.all_to_all(mixed_cols, "mix", split_axis=1, concat_axis=2, tiled=True)
    middle = inputs + mixed.astype(jnp.float32)
    second_full, second_back = jax.vjp(layer_norm, middle, gain_two, shift_two)
    second = second_full.astype(jnp.bfloat16).reshape(rowcount, width)
    inner = jnp.dot(second, chan_in, preferred_element_type=jnp.float32) + chan_inbias
    activ = jax.nn.gelu(inner).astype(jnp.bfloat16)
    branch = jnp.dot(activ, chan_out, preferred_element_type=jnp.float32) + chan_outbias
    mixed_out = (middle + branch.reshape(images, part, width)).astype(jnp.bfloat16)
    live = jnp.arange(images, dtype=jnp.int32) < valid_counts[0]
    upstream = jnp.where(live[:, None, None], out_grad, jnp.zeros_like(out_grad)).reshape(
        rowcount, width
    )
    inner_again = jnp.dot(second, chan_in, preferred_element_type=jnp.float32) + chan_inbias
    activ_full, chan_gelu_back = jax.vjp(jax.nn.gelu, inner_again)
    activ_again = activ_full.astype(jnp.bfloat16)
    grad_chan_out = jnp.einsum(
        "rf,rc->fc", activ_again, upstream, preferred_element_type=jnp.float32
    )
    grad_chan_outbias = jnp.sum(upstream.astype(jnp.float32), axis=0)
    grad_activ = jnp.einsum("rc,fc->rf", upstream, chan_out, preferred_element_type=jnp.float32)
    grad_inner = chan_gelu_back(grad_activ)[0].astype(jnp.bfloat16)
    grad_chan_in = jnp.einsum("rc,rf->cf", second, grad_inner, preferred_element_type=jnp.float32)
    grad_chan_inbias = jnp.sum(grad_inner.astype(jnp.float32), axis=0)
    grad_second = jnp.einsum("rf,cf->rc", grad_inner, chan_in, preferred_element_type=jnp.float32)
    grad_middle, grad_gain_two, grad_shift_two = second_back(
        grad_second.reshape(images, part, width)
    )
    grad_middle = grad_middle + upstream.astype(jnp.float32).reshape(images, part, width)
    grad_cols = lax.all_to_all(
        grad_middle.astype(jnp.bfloat16), "mix", split_axis=2, concat_axis=1, tiled=True
    )
    widened_again = (
        jnp.einsum("bsc,sk->bkc", columns, tok_in, preferred_element_type=jnp.float32)
        + tok_inbias[None, :, None]
    )
    hidden_full, tok_gelu_back = jax.vjp(jax.nn.gelu, widened_again)
    hidden_again = hidden_full.astype(jnp.bfloat16)
    grad_tok_out = jnp.einsum(
        "bkc,bsc->ks", hidden_again, grad_cols, preferred_element_type=jnp.float32
    )
    grad_tok_outbias = jnp.sum(grad_cols.astype(jnp.float32), axis=(0, 2))
    grad_hidden = jnp.einsum("ks,bsc->bkc", tok_out, grad_cols, preferred_element_type=jnp.float32)
    grad_widened = tok_gelu_back(grad_hidden)[0].astype(jnp.bfloat16)
    grad_tok_in = jnp.einsum(
        "bsc,bkc->sk", columns, grad_widened, preferred_element_type=jnp.float32
    )
    grad_tok_inbias = jnp.sum(grad_widened.astype(jnp.float32), axis=(0, 2))
    grad_columns = jnp.einsum(
        "sk,bkc->bsc", tok_in, grad_widened, preferred_element_type=jnp.float32
    ).astype(jnp.bfloat16)
    grad_normed = lax.all_to_all(grad_columns, "mix", split_axis=1, concat_axis=2, tiled=True)
    grad_inputs, grad_gain_one, grad_shift_one = first_back(grad_normed.astype(jnp.float32))
    patch_grad = (grad_middle + grad_inputs).astype(jnp.bfloat16)
    summed = lax.psum(
        (
            grad_gain_one,
            grad_shift_one,
            grad_tok_in,
            grad_tok_inbias,
            grad_tok_out,
            grad_tok_outbias,
            grad_gain_two,
            grad_shift_two,
            grad_chan_in,
            grad_chan_inbias,
            grad_chan_out,
            grad_chan_outbias,
        ),
        ("dp", "mix"),
    )
    return (
        mixed_out,
        patch_grad,
        summed[0],
        summed[1],
        summed[2],
        summed[3],
        summed[4],
        summed[5],
        summed[6],
        summed[7],
        summed[8],
        summed[9],
        summed[10],
        summed[11],
    )


def solution(mesh):
    return jax.shard_map(
        shards,
        mesh=mesh,
        in_specs=(
            P("dp", "mix", None),
            P("dp"),
            P(),
            P(),
            P(),
            P(),
            P(),
            P(),
            P(),
            P(),
            P(),
            P(),
            P(),
            P(),
            P("dp", "mix", None),
        ),
        out_specs=(
            P("dp", "mix", None),
            P("dp", "mix", None),
            P(),
            P(),
            P(),
            P(),
            P(),
            P(),
            P(),
            P(),
            P(),
            P(),
            P(),
            P(),
        ),
        check_vma=False,
    )
```

profile of v0, /device:TPU:0, one launch (start us, length us, event | category | flops | bytes accessed | tf_op | source)
XLA Modules:
  0.0 723.8 jit_solution(6114710992727440725)
XLA Ops:
  15.3 11.4 %copy.67 = bf16[28,49,768]{1,0,2:T(8,128)(2,1)} copy(bf16[28,49,768]{2,1,0:T(8,128)(2,1)} %fusion.25) | data formatting | bytes 4214784 | tf_op jit(solution)/shard_map/convert_element_type | solution.py:36
  26.7 11.5 %reshape.138 = bf16[4,2,131712]{2,1,0:T(2,128)(2,1)} reshape(bf16[768,28,49]{2,1,0:T(8,128)(2,1)} %bitcast.86) | data formatting | bytes 4214784
  38.2 31.3 %all_to_all.54 = bf16[4,2,131712]{2,1,0:T(2,128)(2,1)} all-to-all(bf16[4,2,131712]{2,1,0:T(2,128)(2,1)} %reshape.138), channel_id=1, replica_groups=mesh['dp'=8,'mix'=4] {'mix'}, dimensions={0} | all-to-all | bytes 4214784 | tf_op jit(solution)/shard_map/all_to_all | solution.py:37
  69.6 11.9 %reshape.139 = bf16[768,28,49]{2,1,0:T(8,128)(2,1)} reshape(bf16[4,2,131712]{2,1,0:T(2,128)(2,1)} %all_to_all.54) | data formatting | bytes 4214784
  81.5 9.6 %copy.68 = bf16[28,49,4,192]{3,1,2,0:T(8,128)(2,1)} copy(bf16[28,49,4,192]{1,0,3,2:T(8,128)(2,1)} %bitcast.84) | data formatting | bytes 4214784 | tf_op jit(solution)/shard_map/all_to_all | solution.py:37
  96.8 7.8 %fusion.17 = (bf16[28,384,192]{1,2,0:T(8,128)(2,1)S(1)}, f32[28,192,384]{2,1,0:T(8,128)}) fusion(f32[384]{0:T(512)S(1)} %copy-done.29, bf16[28,196,192]{2,1,0:T(8,128)(2,1)} %all_to_all.43, bf16[196,384]{1,0:T(8,128)(2,1)S(1)} %copy-done), kind=kOutput, calls=%fused_computation.26 | convolution fusion | flops 829882368 | bytes 14645760 | tf_op jit(solution)/shard_map/bsc,sk->bkc/dot_general | solution.py:39
  131.1 28.5 %all-to-all-done.1 = bf16[28,196,192]{2,0,1:T(8,128)(2,1)} async-done(((bf16[28,196,192]{2,0,1:T(8,128)(2,1)}), bf16[28,196,192]{2,0,1:T(8,128)(2,1)}, u32[]{:S(2)}, u32[]{:S(2)}) %all-to-all-start.1) | async-done | bytes 2107424 | tf_op jit(solution)/shard_map/all_to_all | solution.py:47
  186.6 7.7 %reshape.130 = f32[28,49,768]{2,1,0:T(8,128)} reshape(f32[28,49,4,192]{3,2,1,0:T(4,128)} %copy.73) | data formatting | bytes 8429568 | tf_op jit(solution)/shard_map/convert_element_type | solution.py:48
  202.4 17.7 %multiply_convert_fusion = (bf16[1372,3072]{1,0:T(8,128)(2,1)}, f32[1372,3072]{1,0:T(8,128)}) fusion(f32[3072]{0:T(1024)S(1)} %copy-done.27, bf16[1372,768]{1,0:T(8,128)(2,1)} %reshape.126, bf16[768,3072]{1,0:T(8,128)(2,1)} %param.25), kind=kOutput, calls=%fused_computation.10 | convolution fusion | flops 6516056064 | bytes 32126976 | tf_op jit(solution)/shard_map/dot_general | solution.py:51
  220.2 19.9 %convert_reduce_fusion = (f32[3072]{0:T(1024)S(1)}, bf16[1372,3072]{1,0:T(8,128)(2,1)S(1)}) fusion(f32[1372,3072]{1,0:T(8,128)} %get-tuple-element.40, f32[3072]{0:T(1024)S(1)} %copy-done.27, bf16[1372,768]{1,0:T(8,128)(2,1)S(1)} %copy-done.11, bf16[3072,768]{1,0:T(8,128)(2,1)} %param.27), kind=kOutput, calls=%fused_computation.9 | convolution fusion | flops 6570845184 | bytes 32139264 | tf_op jit(solution)/shard_map/rc,fc->rf/dot_general | solution.py:66
  240.1 8.3 %fusion.41 = (f32[768]{0:T(1024)S(1)}, f32[1372,768]{1,0:T(8,128)}) fusion(bf16[1372,3072]{1,0:T(8,128)(2,1)S(1)} %get-tuple-element.46, bf16[768,3072]{1,0:T(8,128)(2,1)S(1)} %bitcast.92), kind=kOutput, calls=%fused_computation.81 | convolution fusion | flops 6474960896 | bytes 17366016 | tf_op jit(solution)/shard_map/rf,cf->rc/dot_general | solution.py:70
  258.3 12.2 %convolution_add_fusion = f32[1372,768]{1,0:T(8,128)} fusion(bf16[1372,3072]{1,0:T(8,128)(2,1)} %get-tuple-element.39, bf16[3072,768]{1,0:T(8,128)(2,1)} %param.27, f32[768]{0:T(1024)S(1)} %copy-done.28), kind=kOutput, calls=%fused_computation.54 | convolution fusion | flops 6474961920 | bytes 17366016 | tf_op jit(solution)/shard_map/dot_general | solution.py:53
  285.9 10.8 %copy.74 = bf16[28,49,768]{1,0,2:T(8,128)(2,1)} copy(bf16[28,49,768]{2,1,0:T(8,128)(2,1)S(1)} %fusion.29) | data formatting | bytes 4214784 | tf_op jit(solution)/shard_map/convert_element_type | solution.py:76
  296.8 11.5 %reshape.140 = bf16[4,2,131712]{2,1,0:T(2,128)(2,1)} reshape(bf16[768,28,49]{2,1,0:T(8,128)(2,1)} %bitcast.87) | data formatting | bytes 4214784
  312.0 13.2 %fusion.43 = f32[3072,768]{1,0:T(8,128)} fusion(bf16[1372,3072]{1,0:T(8,128)(2,1)} %get-tuple-element.39, bf16[1372,768]{1,0:T(8,128)(2,1)} %reshape.128), kind=kOutput, calls=%fused_computation.83 | convolution fusion | flops 6473908224 | bytes 19974144 | tf_op jit(solution)/shard_map/rf,rc->fc/dot_general | solution.py:62
  325.1 12.2 %fusion.42 = f32[768,3072]{1,0:T(8,128)} fusion(bf16[1372,768]{1,0:T(8,128)(2,1)S(1)} %copy-done.12, bf16[1372,3072]{1,0:T(8,128)(2,1)} %copy-done.33), kind=kOutput, calls=%fused_computation.82 | convolution fusion | flops 6473908224 | bytes 19974144 | tf_op jit(solution)/shard_map/rc,rf->cf/dot_general | solution.py:68
  337.7 10.9 %reshape.141 = bf16[768,28,49]{2,1,0:T(8,128)(2,1)} reshape(bf16[4,2,131712]{2,1,0:T(2,128)(2,1)S(1)} %all-to-all-done.2) | data formatting | bytes 4214784
  348.6 8.6 %copy.75 = bf16[28,49,4,192]{3,1,2,0:T(8,128)(2,1)S(1)} copy(bf16[28,49,4,192]{1,0,3,2:T(8,128)(2,1)} %bitcast.85) | data formatting | bytes 4214784 | tf_op jit(solution)/shard_map/all_to_all | solution.py:75
  365.4 9.6 %convert_reduce_fusion.1 = (f32[384]{0:T(512)S(1)}, bf16[28,384,192]{1,2,0:T(8,128)(2,1)S(1)}) fusion(f32[28,192,384]{2,1,0:T(8,128)} %get-tuple-element.38, f32[384]{0:T(512)S(1)} %copy-done.30, bf16[28,196,192]{2,1,0:T(8,128)(2,1)S(1)} %copy-done.10, bf16[384,196]{0,1:T(8,128)(2,1)S(1)} %copy-done.26), kind=kOutput, calls=%fused_computation.27 | convolution fusion | flops 856718976 | bytes 14647296 | tf_op jit(solution)/shard_map/ks,bsc->bkc/dot_general | solution.py:88
  397.5 55.4 %all-to-all-done.3 = bf16[28,196,192]{2,0,1:T(8,128)(2,1)} async-done(((bf16[28,196,192]{2,0,1:T(8,128)(2,1)}), bf16[28,196,192]{2,0,1:T(8,128)(2,1)}, u32[]{:S(2)}, u32[]{:S(2)}) %all-to-all-start.3) | async-done | bytes 2107424 | tf_op jit(solution)/shard_map/all_to_all | solution.py:97
  478.2 8.0 %reshape.131 = f32[28,49,768]{2,1,0:T(8,128)} reshape(f32[28,49,4,192]{3,2,1,0:T(4,128)} %copy.80) | data formatting | bytes 8429568 | tf_op jit(solution)/shard_map/convert_element_type | solution.py:98
  496.2 42.5 %all-reduce = (f32[768]{0:T(1024)}, f32[768]{0:T(1024)}, f32[384]{0:T(512)}, f32[196]{0:T(256)}, f32[768]{0:T(1024)}, /*index=5*/f32[768]{0:T(1024)}, f32[3072]{0:T(1024)}, f32[768]{0:T(1024)}) all-reduce(f32[768]{0:T(1024)S(1)} %get-tuple-element.16, f32[768]{0:T(1024)S(1)} %reduce_sum.199, ...), channel_id=1, replica_groups=mesh['dp'=8,'mix'=4] {'dp','mix'}, use_global_device_ids=true, to_apply=%region_9.10 | all-reduce | flops 7492 | bytes 59936 | tf_op jit(solution)/shard_map/psum | solution.py:100
  545.4 155.2 %all-reduce.4.cloned.1.call-done = (f32[196,384]{1,0:T(8,128)}, f32[384,196]{0,1:T(8,128)}, f32[768,3072]{1,0:T(8,128)}, f32[3072,768]{1,0:T(8,128)}) async-done(((f32[196,384]{1,0:T(8,128)}, f32[384,196]{0,1:T(8,128)}, f32[768,3072]{1,0:T(8,128)}, f32[3072,768]{1,0:T(8,128)}), (f32[196,384]{1,0:T(8,128)}, f32[384,196]{0,1:T(8,128)}, f32[768,3072]{1,0:T(8,128)}, ...) | async-done | bytes 19476496 | tf_op jit(solution)/shard_map/psum | solution.py:100
  704.2 8.8 %copy.95 = f32[768,3072]{1,0:T(8,128)} copy(f32[768,3072]{1,0:T(8,128)} %get-tuple-element.57) | data formatting | bytes 18874368
  (138 shorter events, 183.8 us)
Async XLA Ops:
  7.2 89.6 %copy-start = (bf16[196,384]{1,0:T(8,128)(2,1)S(1)}, bf16[196,384]{1,0:T(8,128)(2,1)}, u32[]{:S(2)}) copy-start(bf16[196,384]{1,0:T(8,128)(2,1)} %param.19) | copy-start | bytes 451588
  7.2 6.0 copy-start.2
  7.2 6.0 copy-start.19
  7.2 6.0 copy-start.23
  96.8 9.8 %copy-start.25 = (bf16[384,196]{0,1:T(8,128)(2,1)S(1)}, bf16[384,196]{0,1:T(8,128)(2,1)}, u32[]{:S(2)}) copy-start(bf16[384,196]{0,1:T(8,128)(2,1)} %param.21) | copy-start | bytes 451588
  96.8 9.8 %copy-start.31 = (f32[196]{0:T(256)S(1)}, f32[196]{0:T(256)}, u32[]{:S(2)}) copy-start(f32[196]{0:T(256)} %param.22) | copy-start | bytes 2356
  117.1 42.5 %all-to-all-start.1 = ((bf16[28,196,192]{2,0,1:T(8,128)(2,1)}), bf16[28,196,192]{2,0,1:T(8,128)(2,1)}, u32[]{:S(2)}, u32[]{:S(2)}) async-start(bf16[28,196,192]{2,0,1:T(8,128)(2,1)} %copy.70), calls=%async_computation.1 | async-start | bytes 6422528 | tf_op jit(solution)/shard_map/all_to_all | solution.py:47
  202.4 17.7 %copy-start.11 = (bf16[1372,768]{1,0:T(8,128)(2,1)S(1)}, bf16[1372,768]{1,0:T(8,128)(2,1)}, u32[]{:S(2)}) copy-start(bf16[1372,768]{1,0:T(8,128)(2,1)} %reshape.128) | copy-start | bytes 6322180
  202.4 37.7 %slice-start.3 = ((s8[4718592]{0:T(1024)(128)(4,1)}), s8[4194304]{0:T(1024)(128)(4,1)S(1)}, s32[]{:S(2)}) async-start(s8[4718592]{0:T(1024)(128)(4,1)} %bitcast.91), calls=%async_computation.8 | async-start | bytes 8388608
  220.2 20.0 %slice-start.4 = ((s8[4718592]{0:T(1024)(128)(4,1)}), s8[524288]{0:T(1024)(128)(4,1)S(1)}, s32[]{:S(2)}) async-start(s8[4718592]{0:T(1024)(128)(4,1)} %bitcast.91), calls=%async_computation.9 | async-start | bytes 1048576
  240.1 8.4 %copy-start.33 = (bf16[1372,3072]{1,0:T(8,128)(2,1)}, bf16[1372,3072]{1,0:T(8,128)(2,1)S(1)}, u32[]{:S(2)}) copy-start(bf16[1372,3072]{1,0:T(8,128)(2,1)S(1)} %get-tuple-element.46) | copy-start | bytes 25288708
  275.8 9.6 %copy-start.6 = (bf16[28,49,768]{2,1,0:T(8,128)(2,1)S(1)}, bf16[28,49,768]{2,1,0:T(8,128)(2,1)}, u32[]{:S(2)}) copy-start(bf16[28,49,768]{2,1,0:T(8,128)(2,1)} %get-tuple-element.31) | copy-start | bytes 6322180
  308.3 29.4 %all-to-all-start.2 = ((bf16[4,2,131712]{2,1,0:T(2,128)(2,1)}), bf16[4,2,131712]{2,1,0:T(2,128)(2,1)S(1)}, u32[]{:S(2)}, u32[]{:S(2)}) async-start(bf16[4,2,131712]{2,1,0:T(2,128)(2,1)} %reshape.140), calls=%async_computation.2 | async-start | bytes 4214784 | tf_op jit(solution)/shard_map/all_to_all | solution.py:75
  311.9 388.7 %all-reduce.4.cloned.1.call-start = ((), (), s32[]{:S(2)}) async-start(), calls=%async_computation.4 | async-start | bytes 38977536 | tf_op jit(solution)/shard_map/psum | solution.py:100
  311.9 13.2 %copy-start.12 = (bf16[1372,768]{1,0:T(8,128)(2,1)S(1)}, bf16[1372,768]{1,0:T(8,128)(2,1)}, u32[]{:S(2)}) copy-start(bf16[1372,768]{1,0:T(8,128)(2,1)} %reshape.126) | copy-start | bytes 6322180
  365.4 11.7 %copy-start.9 = (bf16[28,196,192]{2,1,0:T(8,128)(2,1)S(1)}, bf16[28,196,192]{2,1,0:T(8,128)(2,1)}, u32[]{:S(2)}) copy-start(bf16[28,196,192]{2,1,0:T(8,128)(2,1)} %all_to_all.43) | copy-start | bytes 6322180
  392.1 60.8 %all-to-all-start.3 = ((bf16[28,196,192]{2,0,1:T(8,128)(2,1)}), bf16[28,196,192]{2,0,1:T(8,128)(2,1)}, u32[]{:S(2)}, u32[]{:S(2)}) async-start(bf16[28,196,192]{2,0,1:T(8,128)(2,1)} %copy.77), calls=%async_computation.3 | async-start | bytes 6422528 | tf_op jit(solution)/shard_map/all_to_all | solution.py:97
  459.9 10.8 %copy-start.7 = (bf16[28,196,192]{1,2,0:T(8,128)(2,1)}, bf16[28,196,192]{1,2,0:T(8,128)(2,1)S(1)}, u32[]{:S(2)}) copy-start(bf16[28,196,192]{1,2,0:T(8,128)(2,1)S(1)} %copy.78) | copy-start | bytes 6322180
  478.2 10.5 %copy-start.3 = (bf16[28,49,768]{2,1,0:T(8,128)(2,1)S(1)}, bf16[28,49,768]{2,1,0:T(8,128)(2,1)}, u32[]{:S(2)}) copy-start(bf16[28,49,768]{2,1,0:T(8,128)(2,1)} %param.15) | copy-start | bytes 6322180
  478.2 10.5 %copy-start.14 = (f32[28,49]{1,0:T(8,128)S(1)}, f32[28,49]{1,0:T(8,128)}, u32[]{:S(2)}) copy-start(f32[28,49]{1,0:T(8,128)} %copy-done.13) | copy-start | bytes 16468
  478.2 10.5 %copy-start.20 = (f32[768]{0:T(1024)S(1)}, f32[768]{0:T(1024)}, u32[]{:S(2)}) copy-start(f32[768]{0:T(1024)} %param.17) | copy-start | bytes 9220
  702.3 10.6 %slice-start = ((s8[9437184]{0:T(1024)(128)(4,1)}), s8[4194304]{0:T(1024)(128)(4,1)S(1)}, s32[]{:S(2)}) async-start(s8[9437184]{0:T(1024)(128)(4,1)} %bitcast.89), calls=%async_computation.5 | async-start | bytes 8388608
  704.2 8.8 %slice-start.1 = ((s8[9437184]{0:T(1024)(128)(4,1)}), s8[4194304]{0:T(1024)(128)(4,1)S(1)}, s32[]{:S(2)}) async-start(s8[9437184]{0:T(1024)(128)(4,1)} %bitcast.89), calls=%async_computation.6 | async-start | bytes 8388608
  704.2 8.8 %slice-start.2 = ((s8[9437184]{0:T(1024)(128)(4,1)}), s8[1048576]{0:T(1024)(128)(4,1)S(1)}, s32[]{:S(2)}) async-start(s8[9437184]{0:T(1024)(128)(4,1)} %bitcast.89), calls=%async_computation.7 | async-start | bytes 2097152
  (19 other events, 62.7 us)
Sparse Core Ops, SparseCore 0:
  379.3 321.2 all-reduce.3
where the time goes:
time: 731 us; the launch traced here: 724 us
  waiting for transfers between devices  239 us (33%)
  local copies, waits for them, and re-layouts  220 us (30%)
  matrix products  117 us (16%)
  blocking collectives  73.8 us (10%)
  other arithmetic  44.7 us (6%)
  between operations  15.3 us (2%)
  starting transfers between devices  13.2 us (2%)
    psum x1, waiting for transfers between devices, shards(): lax.psum((grad_gain_one, grad_shift_one, grad_tok_in, grad_tok_inbias, gr...  155 us
    unnamed x86, local copies, waits for them, and re-layouts  71.9 us
    all_to_all x1, waiting for transfers between devices, shards(): lax.all_to_all(grad_columns, 'mix', split_axis=1, concat_axis=2, tiled=True)  55.4 us
    psum x1, blocking collectives, shards(): lax.psum((grad_gain_one, grad_shift_one, grad_tok_in, grad_tok_inbias, gr...  42.5 us
    all_to_all x1, blocking collectives, shards(): lax.all_to_all(normed, 'mix', split_axis=2, concat_axis=1, tiled=True)  31.3 us
    all_to_all x1, waiting for transfers between devices, shards(): lax.all_to_all(mixed_cols, 'mix', split_axis=1, concat_axis=2, tiled=True)  28.5 us
    convert_element_type x4, local copies, waits for them, and re-layouts, shards(): middle = inputs + mixed.astype(jnp.float32)  27.2 us
    convert_element_type x4, local copies, waits for them, and re-layouts, shards(): grad_normed.astype(jnp.float32)  26.3 us
  transfers between devices with their start and end apart: 4, of which 4 were waited for; matrix products, arithmetic and copies ran while one was open for 13% of the time, Pallas kernels for 0%

commit v1 on v0

--- a/solution.py
+++ b/solution.py
@@ -34,7 +34,10 @@
     inputs = patches.astype(jnp.float32)
     normed_full, first_back = jax.vjp(layer_norm, inputs, gain_one, shift_one)
     normed = normed_full.astype(jnp.bfloat16)
-    columns = lax.all_to_all(normed, "mix", split_axis=2, concat_axis=1, tiled=True)
+    columns = jnp.concatenate(
+        lax.all_to_all(jnp.stack(jnp.split(normed, lax.axis_size("mix"), axis=2)), "mix", 0, 0),
+        axis=1,
+    )
     widened = (
         jnp.einsum("bsc,sk->bkc", columns, tok_in, preferred_element_type=jnp.float32)
         + tok_inbias[None, :, None]

time: 731 us -> 700 us (0.958)
  local copies, waits for them, and re-layouts: 220 us -> 179 us
  blocking collectives: 73.8 us -> 84.1 us
    unnamed x86 -> x84, local copies, waits for them, and re-layouts: 71.9 us -> 48.4 us
    all_to_all x2 -> x0, local copies, waits for them, and re-layouts: 15.3 us -> none  [shards(): lax.all_to_all(normed, 'mix', split_axis=2, concat_axis=1, tiled=True)]
    convert_element_type x1 -> x0, local copies, waits for them, and re-layouts: 11.4 us -> none  [shards(): normed = normed_full.astype(jnp.bfloat16)]
    all_to_all x1, blocking collectives: 31.3 us -> 41.6 us  [shards(): lax.all_to_all(jnp.stack(jnp.split(normed, lax.axis_size('mix'), axis=2))...]
    reshape x0 -> x2, local copies, waits for them, and re-layouts: none -> 7.8 us  [shards(): jnp.concatenate(lax.all_to_all(jnp.stack(jnp.split(normed, lax.axis_size(...]
  transfers between devices with their start and end apart: 4 -> 4, of which waited for: 4 -> 3; matrix products, arithmetic and copies ran while one was open for 13% -> 14% of each run, Pallas kernels for 0% -> 0%
where the time goes in v1:
time: 700 us; the launch traced here: 692 us
  waiting for transfers between devices  239 us (34%)
  local copies, waits for them, and re-layouts  179 us (26%)
  matrix products  117 us (17%)
  blocking collectives  84.1 us (12%)
  other arithmetic  44.6 us (6%)
  between operations  15.3 us (2%)
  starting transfers between devices  13.5 us (2%)
    psum x1, waiting for transfers between devices, shards(): lax.psum((grad_gain_one, grad_shift_one, grad_tok_in, grad_tok_inbias, gr...  155 us
    all_to_all x1, waiting for transfers between devices, shards(): lax.all_to_all(grad_columns, 'mix', split_axis=1, concat_axis=2, tiled=True)  54.8 us
    unnamed x84, local copies, waits for them, and re-layouts  48.4 us
    psum x1, blocking collectives, shards(): lax.psum((grad_gain_one, grad_shift_one, grad_tok_in, grad_tok_inbias, gr...  42.5 us
    all_to_all x1, blocking collectives, shards(): lax.all_to_all(jnp.stack(jnp.split(normed, lax.axis_size('mix'), axis=2))...  41.6 us
    all_to_all x1, waiting for transfers between devices, shards(): lax.all_to_all(mixed_cols, 'mix', split_axis=1, concat_axis=2, tiled=True)  28.5 us
    convert_element_type x4, local copies, waits for them, and re-layouts, shards(): middle = inputs + mixed.astype(jnp.float32)  27.2 us
    convert_element_type x4, local copies, waits for them, and re-layouts, shards(): grad_normed.astype(jnp.float32)  26.3 us
  transfers between devices with their start and end apart: 4, of which 3 were waited for; matrix products, arithmetic and copies ran while one was open for 14% of the time, Pallas kernels for 0%

profile of v1, /device:TPU:0, one launch (start us, length us, event | category | flops | bytes accessed | tf_op | source)
XLA Modules:
  0.0 691.9 jit_solution(12507294120680327198)
XLA Ops:
  16.0 41.6 %all_to_all.41 = bf16[4,28,49,192]{3,2,1,0:T(8,128)(2,1)S(1)} all-to-all(bf16[4,28,49,192]{3,2,1,0:T(8,128)(2,1)S(1)} %pad_maximum_fusion), channel_id=1, replica_groups=mesh['dp'=8,'mix'=4] {'mix'}, dimensions={0} | all-to-all | bytes 4214784 | tf_op jit(solution)/shard_map/all_to_all | solution.py:38
  65.4 7.9 %fusion.17 = (bf16[28,384,192]{1,2,0:T(8,128)(2,1)S(1)}, f32[28,192,384]{2,1,0:T(8,128)}) fusion(f32[384]{0:T(512)S(1)} %copy-done.29, bf16[28,196,192]{2,1,0:T(8,128)(2,1)} %reshape.133, bf16[196,384]{1,0:T(8,128)(2,1)S(1)} %copy-done), kind=kOutput, calls=%fused_computation.26 | convolution fusion | flops 829882368 | bytes 14645760 | tf_op jit(solution)/shard_map/bsc,sk->bkc/dot_general | solution.py:42
  100.1 28.5 %all-to-all-done.1 = bf16[28,196,192]{2,0,1:T(8,128)(2,1)} async-done(((bf16[28,196,192]{2,0,1:T(8,128)(2,1)}), bf16[28,196,192]{2,0,1:T(8,128)(2,1)}, u32[]{:S(2)}, u32[]{:S(2)}) %all-to-all-start.1) | async-done | bytes 2107424 | tf_op jit(solution)/shard_map/all_to_all | solution.py:50
  128.6 7.5 %copy.69 = bf16[28,196,192]{1,2,0:T(8,128)(2,1)} copy(bf16[28,196,192]{2,0,1:T(8,128)(2,1)} %all-to-all-done.1) | data formatting | bytes 4214784 | tf_op jit(solution)/shard_map/all_to_all | solution.py:50
  148.1 7.5 %copy.71 = f32[28,49,4,192]{3,2,1,0:T(4,128)} copy(f32[28,49,4,192]{3,1,2,0:T(8,128)} %bitcast.87) | data formatting | bytes 8429568 | tf_op jit(solution)/shard_map/convert_element_type | solution.py:51
  155.6 7.7 %reshape.138 = f32[28,49,768]{2,1,0:T(8,128)} reshape(f32[28,49,4,192]{3,2,1,0:T(4,128)} %copy.71) | data formatting | bytes 8429568 | tf_op jit(solution)/shard_map/convert_element_type | solution.py:51
  171.3 17.7 %multiply_convert_fusion = (bf16[1372,3072]{1,0:T(8,128)(2,1)}, f32[1372,3072]{1,0:T(8,128)}) fusion(f32[3072]{0:T(1024)S(1)} %copy-done.27, bf16[1372,768]{1,0:T(8,128)(2,1)} %reshape.134, bf16[768,3072]{1,0:T(8,128)(2,1)} %param.25), kind=kOutput, calls=%fused_computation.10 | convolution fusion | flops 6516056064 | bytes 32126976 | tf_op jit(solution)/shard_map/dot_general | solution.py:54
  189.0 19.9 %convert_reduce_fusion = (f32[3072]{0:T(1024)S(1)}, bf16[1372,3072]{1,0:T(8,128)(2,1)S(1)}) fusion(f32[1372,3072]{1,0:T(8,128)} %get-tuple-element.44, f32[3072]{0:T(1024)S(1)} %copy-done.27, bf16[1372,768]{1,0:T(8,128)(2,1)S(1)} %copy-done.11, bf16[3072,768]{1,0:T(8,128)(2,1)} %param.27), kind=kOutput, calls=%fused_computation.9 | convolution fusion | flops 6570845184 | bytes 32139264 | tf_op jit(solution)/shard_map/rc,fc->rf/dot_general | solution.py:69
  209.0 8.3 %fusion.41 = (f32[768]{0:T(1024)S(1)}, f32[1372,768]{1,0:T(8,128)}) fusion(bf16[1372,3072]{1,0:T(8,128)(2,1)S(1)} %get-tuple-element.50, bf16[768,3072]{1,0:T(8,128)(2,1)S(1)} %bitcast.95), kind=kOutput, calls=%fused_computation.86 | convolution fusion | flops 6474960896 | bytes 17366016 | tf_op jit(solution)/shard_map/rf,cf->rc/dot_general | solution.py:73
  227.2 12.1 %convolution_add_fusion = f32[1372,768]{1,0:T(8,128)} fusion(bf16[1372,3072]{1,0:T(8,128)(2,1)} %get-tuple-element.43, bf16[3072,768]{1,0:T(8,128)(2,1)} %param.27, f32[768]{0:T(1024)S(1)} %copy-done.28), kind=kOutput, calls=%fused_computation.54 | convolution fusion | flops 6474961920 | bytes 17366016 | tf_op jit(solution)/shard_map/dot_general | solution.py:56
  254.6 10.8 %copy.72 = bf16[28,49,768]{1,0,2:T(8,128)(2,1)} copy(bf16[28,49,768]{2,1,0:T(8,128)(2,1)S(1)} %fusion.29) | data formatting | bytes 4214784 | tf_op jit(solution)/shard_map/convert_element_type | solution.py:79
  265.5 11.5 %reshape.146 = bf16[4,2,131712]{2,1,0:T(2,128)(2,1)} reshape(bf16[768,28,49]{2,1,0:T(8,128)(2,1)} %bitcast.90) | data formatting | bytes 4214784
  280.6 13.5 %fusion.43 = f32[3072,768]{1,0:T(8,128)} fusion(bf16[1372,3072]{1,0:T(8,128)(2,1)} %get-tuple-element.43, bf16[1372,768]{1,0:T(8,128)(2,1)} %reshape.136), kind=kOutput, calls=%fused_computation.88 | convolution fusion | flops 6473908224 | bytes 19974144 | tf_op jit(solution)/shard_map/rf,rc->fc/dot_general | solution.py:65
  294.1 12.2 %fusion.42 = f32[768,3072]{1,0:T(8,128)} fusion(bf16[1372,768]{1,0:T(8,128)(2,1)S(1)} %copy-done.12, bf16[1372,3072]{1,0:T(8,128)(2,1)} %copy-done.33), kind=kOutput, calls=%fused_computation.87 | convolution fusion | flops 6473908224 | bytes 19974144 | tf_op jit(solution)/shard_map/rc,rf->cf/dot_general | solution.py:71
  306.4 10.9 %reshape.147 = bf16[768,28,49]{2,1,0:T(8,128)(2,1)} reshape(bf16[4,2,131712]{2,1,0:T(2,128)(2,1)S(1)} %all-to-all-done.2) | data formatting | bytes 4214784
  317.3 8.6 %copy.73 = bf16[28,49,4,192]{3,1,2,0:T(8,128)(2,1)S(1)} copy(bf16[28,49,4,192]{1,0,3,2:T(8,128)(2,1)} %bitcast.89) | data formatting | bytes 4214784 | tf_op jit(solution)/shard_map/all_to_all | solution.py:78
  334.1 9.6 %convert_reduce_fusion.1 = (f32[384]{0:T(512)S(1)}, bf16[28,384,192]{1,2,0:T(8,128)(2,1)S(1)}) fusion(f32[28,192,384]{2,1,0:T(8,128)} %get-tuple-element.42, f32[384]{0:T(512)S(1)} %copy-done.30, bf16[28,196,192]{2,1,0:T(8,128)(2,1)S(1)} %copy-done.10, bf16[384,196]{0,1:T(8,128)(2,1)S(1)} %copy-done.26), kind=kOutput, calls=%fused_computation.27 | convolution fusion | flops 856718976 | bytes 14647296 | tf_op jit(solution)/shard_map/ks,bsc->bkc/dot_general | solution.py:91
  353.2 7.5 %copy.75 = bf16[28,196,192]{2,0,1:T(8,128)(2,1)} copy(bf16[28,196,192]{1,2,0:T(8,128)(2,1)} %convert_bitcast_fusion) | data formatting | bytes 4214784 | tf_op jit(solution)/shard_map/convert_element_type | solution.py:99
  366.2 54.8 %all-to-all-done.3 = bf16[28,196,192]{2,0,1:T(8,128)(2,1)} async-done(((bf16[28,196,192]{2,0,1:T(8,128)(2,1)}), bf16[28,196,192]{2,0,1:T(8,128)(2,1)}, u32[]{:S(2)}, u32[]{:S(2)}) %all-to-all-start.3) | async-done | bytes 2107424 | tf_op jit(solution)/shard_map/all_to_all | solution.py:100
  438.9 7.5 %copy.78 = f32[28,49,4,192]{3,2,1,0:T(4,128)} copy(f32[28,49,4,192]{3,1,2,0:T(8,128)} %bitcast.88) | data formatting | bytes 8429568 | tf_op jit(solution)/shard_map/convert_element_type | solution.py:101
  446.4 8.0 %reshape.139 = f32[28,49,768]{2,1,0:T(8,128)} reshape(f32[28,49,4,192]{3,2,1,0:T(4,128)} %copy.78) | data formatting | bytes 8429568 | tf_op jit(solution)/shard_map/convert_element_type | solution.py:101
  464.4 42.5 %all-reduce = (f32[768]{0:T(1024)}, f32[768]{0:T(1024)}, f32[384]{0:T(512)}, f32[196]{0:T(256)}, f32[768]{0:T(1024)}, /*index=5*/f32[768]{0:T(1024)}, f32[3072]{0:T(1024)}, f32[768]{0:T(1024)}) all-reduce(f32[768]{0:T(1024)S(1)} %get-tuple-element.16, f32[768]{0:T(1024)S(1)} %reduce_sum.199, ...), channel_id=1, replica_groups=mesh['dp'=8,'mix'=4] {'dp','mix'}, use_global_device_ids=true, to_apply=%region_9.10 | all-reduce | flops 7492 | bytes 59936 | tf_op jit(solution)/shard_map/psum | solution.py:103
  513.6 155.2 %all-reduce.4.cloned.1.call-done = (f32[196,384]{1,0:T(8,128)}, f32[384,196]{0,1:T(8,128)}, f32[768,3072]{1,0:T(8,128)}, f32[3072,768]{1,0:T(8,128)}) async-done(((f32[196,384]{1,0:T(8,128)}, f32[384,196]{0,1:T(8,128)}, f32[768,3072]{1,0:T(8,128)}, f32[3072,768]{1,0:T(8,128)}), (f32[196,384]{1,0:T(8,128)}, f32[384,196]{0,1:T(8,128)}, f32[768,3072]{1,0:T(8,128)}, ...) | async-done | bytes 19476496 | tf_op jit(solution)/shard_map/psum | solution.py:103
  672.3 8.8 %copy.93 = f32[768,3072]{1,0:T(8,128)} copy(f32[768,3072]{1,0:T(8,128)} %get-tuple-element.61) | data formatting | bytes 18874368
  (137 shorter events, 156.5 us)
Async XLA Ops:
  7.2 58.2 %copy-start = (bf16[196,384]{1,0:T(8,128)(2,1)S(1)}, bf16[196,384]{1,0:T(8,128)(2,1)}, u32[]{:S(2)}) copy-start(bf16[196,384]{1,0:T(8,128)(2,1)} %param.19) | copy-start | bytes 451588
  7.2 6.0 copy-start.2
  7.2 6.0 copy-start.19
  57.6 7.8 %copy-start.29 = (f32[384]{0:T(512)S(1)}, f32[384]{0:T(512)}, u32[]{:S(2)}) copy-start(f32[384]{0:T(512)} %param.20) | copy-start | bytes 4612
  65.4 9.8 %copy-start.25 = (bf16[384,196]{0,1:T(8,128)(2,1)S(1)}, bf16[384,196]{0,1:T(8,128)(2,1)}, u32[]{:S(2)}) copy-start(bf16[384,196]{0,1:T(8,128)(2,1)} %param.21) | copy-start | bytes 451588
  65.4 9.8 %copy-start.31 = (f32[196]{0:T(256)S(1)}, f32[196]{0:T(256)}, u32[]{:S(2)}) copy-start(f32[196]{0:T(256)} %param.22) | copy-start | bytes 2356
  85.7 42.8 %all-to-all-start.1 = ((bf16[28,196,192]{2,0,1:T(8,128)(2,1)}), bf16[28,196,192]{2,0,1:T(8,128)(2,1)}, u32[]{:S(2)}, u32[]{:S(2)}) async-start(bf16[28,196,192]{2,0,1:T(8,128)(2,1)} %copy.68), calls=%async_computation.1 | async-start | bytes 6422528 | tf_op jit(solution)/shard_map/all_to_all | solution.py:50
  171.3 17.7 %copy-start.11 = (bf16[1372,768]{1,0:T(8,128)(2,1)S(1)}, bf16[1372,768]{1,0:T(8,128)(2,1)}, u32[]{:S(2)}) copy-start(bf16[1372,768]{1,0:T(8,128)(2,1)} %reshape.136) | copy-start | bytes 6322180
  171.3 37.7 %slice-start.3 = ((s8[4718592]{0:T(1024)(128)(4,1)}), s8[4194304]{0:T(1024)(128)(4,1)S(1)}, s32[]{:S(2)}) async-start(s8[4718592]{0:T(1024)(128)(4,1)} %bitcast.94), calls=%async_computation.8 | async-start | bytes 8388608
  189.0 20.0 %slice-start.4 = ((s8[4718592]{0:T(1024)(128)(4,1)}), s8[524288]{0:T(1024)(128)(4,1)S(1)}, s32[]{:S(2)}) async-start(s8[4718592]{0:T(1024)(128)(4,1)} %bitcast.94), calls=%async_computation.9 | async-start | bytes 1048576
  209.0 8.4 %copy-start.33 = (bf16[1372,3072]{1,0:T(8,128)(2,1)}, bf16[1372,3072]{1,0:T(8,128)(2,1)S(1)}, u32[]{:S(2)}) copy-start(bf16[1372,3072]{1,0:T(8,128)(2,1)S(1)} %get-tuple-element.50) | copy-start | bytes 25288708
  244.4 9.6 %copy-start.6 = (bf16[28,49,768]{2,1,0:T(8,128)(2,1)S(1)}, bf16[28,49,768]{2,1,0:T(8,128)(2,1)}, u32[]{:S(2)}) copy-start(bf16[28,49,768]{2,1,0:T(8,128)(2,1)} %get-tuple-element.31) | copy-start | bytes 6322180
  277.0 29.4 %all-to-all-start.2 = ((bf16[4,2,131712]{2,1,0:T(2,128)(2,1)}), bf16[4,2,131712]{2,1,0:T(2,128)(2,1)S(1)}, u32[]{:S(2)}, u32[]{:S(2)}) async-start(bf16[4,2,131712]{2,1,0:T(2,128)(2,1)} %reshape.146), calls=%async_computation.2 | async-start | bytes 4214784 | tf_op jit(solution)/shard_map/all_to_all | solution.py:78
  280.6 388.2 %all-reduce.4.cloned.1.call-start = ((), (), s32[]{:S(2)}) async-start(), calls=%async_computation.4 | async-start | bytes 38977536 | tf_op jit(solution)/shard_map/psum | solution.py:103
  280.6 13.5 %copy-start.12 = (bf16[1372,768]{1,0:T(8,128)(2,1)S(1)}, bf16[1372,768]{1,0:T(8,128)(2,1)}, u32[]{:S(2)}) copy-start(bf16[1372,768]{1,0:T(8,128)(2,1)} %reshape.134) | copy-start | bytes 6322180
  334.1 11.6 %copy-start.9 = (bf16[28,196,192]{2,1,0:T(8,128)(2,1)S(1)}, bf16[28,196,192]{2,1,0:T(8,128)(2,1)}, u32[]{:S(2)}) copy-start(bf16[28,196,192]{2,1,0:T(8,128)(2,1)} %reshape.133) | copy-start | bytes 6322180
  360.7 60.3 %all-to-all-start.3 = ((bf16[28,196,192]{2,0,1:T(8,128)(2,1)}), bf16[28,196,192]{2,0,1:T(8,128)(2,1)}, u32[]{:S(2)}, u32[]{:S(2)}) async-start(bf16[28,196,192]{2,0,1:T(8,128)(2,1)} %copy.75), calls=%async_computation.3 | async-start | bytes 6422528 | tf_op jit(solution)/shard_map/all_to_all | solution.py:100
  428.0 10.8 %copy-start.7 = (bf16[28,196,192]{1,2,0:T(8,128)(2,1)}, bf16[28,196,192]{1,2,0:T(8,128)(2,1)S(1)}, u32[]{:S(2)}) copy-start(bf16[28,196,192]{1,2,0:T(8,128)(2,1)S(1)} %copy.76) | copy-start | bytes 6322180
  446.4 10.5 %copy-start.3 = (bf16[28,49,768]{2,1,0:T(8,128)(2,1)S(1)}, bf16[28,49,768]{2,1,0:T(8,128)(2,1)}, u32[]{:S(2)}) copy-start(bf16[28,49,768]{2,1,0:T(8,128)(2,1)} %param.15) | copy-start | bytes 6322180
  446.4 10.5 %copy-start.14 = (f32[28,49]{1,0:T(8,128)S(1)}, f32[28,49]{1,0:T(8,128)}, u32[]{:S(2)}) copy-start(f32[28,49]{1,0:T(8,128)} %copy-done.13) | copy-start | bytes 16468
  446.4 10.5 %copy-start.20 = (f32[768]{0:T(1024)S(1)}, f32[768]{0:T(1024)}, u32[]{:S(2)}) copy-start(f32[768]{0:T(1024)} %param.17) | copy-start | bytes 9220
  670.5 10.6 %slice-start = ((s8[9437184]{0:T(1024)(128)(4,1)}), s8[4194304]{0:T(1024)(128)(4,1)S(1)}, s32[]{:S(2)}) async-start(s8[9437184]{0:T(1024)(128)(4,1)} %bitcast.92), calls=%async_computation.5 | async-start | bytes 8388608
  672.3 8.8 %slice-start.1 = ((s8[9437184]{0:T(1024)(128)(4,1)}), s8[4194304]{0:T(1024)(128)(4,1)S(1)}, s32[]{:S(2)}) async-start(s8[9437184]{0:T(1024)(128)(4,1)} %bitcast.92), calls=%async_computation.6 | async-start | bytes 8388608
  672.3 8.8 %slice-start.2 = ((s8[9437184]{0:T(1024)(128)(4,1)}), s8[1048576]{0:T(1024)(128)(4,1)S(1)}, s32[]{:S(2)}) async-start(s8[9437184]{0:T(1024)(128)(4,1)} %bitcast.92), calls=%async_computation.7 | async-start | bytes 2097152
  (19 other events, 62.3 us)
Sparse Core Ops, SparseCore 0:
  347.9 320.7 all-reduce.3
